TPU v7x, 512 devices: a whole 4x8x8 slice. The times are simulated.
512 devices in a mesh: leaf: 16 (over y, core), sub: 32 (over x, z).
Axes of the slice: x: 4, y: 8, z: 8, core: 2. Of those that a mesh axis runs over, the one named last changes fastest.
Arguments:
- panels: bfloat16 [3072, 4, 256, 128], P(('leaf', 'sub')), may hold values from -1 to 1
- root_panels: bfloat16 [3072, 256, 128], P(('leaf', 'sub')), may hold values from -1 to 1
- low_inverse: bfloat16 [3072, 128, 128], P(('leaf', 'sub')), may hold values from -4 to 1.5, as said below
- structure: int32 [3072, 4], P(('leaf', 'sub')), may hold values from 0 to 31, all different within a row; in each aligned block of 6 rows (0 to 5, 6 to 11, ...) at most 2 rows name the same one
- owner_map: int32 [16, 32], replicated, may hold values from 0 to 31, each once within a row
- upper_block: float32 [512, 256, 256], P(('leaf', 'sub')), may hold values from -1 to 10, as said below
- upper_cot: float32 [512, 256, 256], P(('leaf', 'sub')), may hold values from -6 to 6
- root_block: float32 [256, 256], replicated, may hold values from -1 to 10, as said below
- root_cot: float32 [256, 256], replicated, may hold values from -6 to 6
Outputs:
- panel_grad: bfloat16 [3072, 4, 256, 128], P(('leaf', 'sub'))
- root_grad: bfloat16 [3072, 256, 128], P(('leaf', 'sub'))
Inputs may be any that keep to these rules, and one draw needn't show every extreme that they name: `structure`: among the 6 rows of one device no upper supernode is named more than 2 times; the names within a row differ. Each row of owner_map is a permutation of the group's devices. `upper_block`: Symmetric; diagonal from 6 to 10, every off-diagonal entry at most 2 / 256 in size, so that the diagonal dominates its row. `root_block`: Symmetric; diagonal from 8 to 10, every off-diagonal entry at most 1 / 256 in size, so that the diagonal dominates its row. `low_inverse`: lower triangular, diagonal from 0.5 to 1.5.
All inputs are finite; a program needn't handle non-finite values.
Results may differ from a plain program's by a relative error of at most 0.0014.
The roundings to bfloat16 on the way count: a program that leaves them out, or rounds other values in their place, can miss the bound.
Values may be sent and summed in bfloat16 or wider, within the bound.
A program may use at most 64 MiB of HBM per device.

v0:
```python
import jax
import jax.numpy as jnp
from jax import lax
from jax.sharding import PartitionSpec as P


def adjoint_block(schur, cotangent):
    factor = jnp.linalg.cholesky(schur)
    identity = jnp.eye(schur.shape[0], dtype=schur.dtype)
    inverse = jax.scipy.linalg.solve_triangular(factor, identity, lower=True)
    product = jnp.dot(factor.T, cotangent, precision=lax.Precision.HIGHEST)
    lowered = jnp.tril(product) - 0.5 * jnp.diag(jnp.diag(product))
    adjoint_full = jnp.dot(
        jnp.dot(inverse.T, lowered, precision=lax.Precision.HIGHEST),
        inverse,
        precision=lax.Precision.HIGHEST,
    )
    return (0.5 * (adjoint_full + adjoint_full.T)).astype(jnp.bfloat16)


def body(
    panels,
    root_panels,
    low_inverse,
    structure,
    owner_map,
    upper_block,
    upper_cot,
    root_block,
    root_cot,
):
    devices_sub = lax.axis_size("sub")
    rows_dev, blocks_row, height, breadth = panels.shape
    item_count = rows_dev * blocks_row
    capacity = max(2, 2 * item_count // devices_sub)
    group_id = lax.axis_index("leaf")
    owners = lax.dynamic_index_in_dim(owner_map, group_id, 0, keepdims=False)
    target = jnp.take(owners, structure.reshape(item_count))
    onehot = (target[:, None] == jnp.arange(devices_sub, dtype=jnp.int32)[None, :]).astype(
        jnp.int32
    )
    earlier = jnp.cumsum(onehot, axis=0) - onehot
    slot_id = jnp.sum(earlier * onehot, axis=1)
    position = target * capacity + slot_id
    flat_panels = panels.reshape(item_count, height, breadth)
    outgoing = (
        jnp.zeros((devices_sub * capacity, height, breadth), jnp.bfloat16)
        .at[position]
        .set(flat_panels)
    )
    incoming = lax.all_to_all(outgoing, "sub", split_axis=0, concat_axis=0, tiled=True)
    gram_sum = jnp.einsum("nbw,ncw->bc", incoming, incoming, preferred_element_type=jnp.float32)
    upper_adjoint = adjoint_block(upper_block[0] - gram_sum, upper_cot[0])
    answer = (
        -2.0
        * jnp.einsum("bc,ncw->nbw", upper_adjoint, incoming, preferred_element_type=jnp.float32)
    ).astype(jnp.bfloat16)
    returned = lax.all_to_all(answer, "sub", split_axis=0, concat_axis=0, tiled=True)
    panel_adjoint = returned[position]
    panel_adjoint = panel_adjoint.reshape(rows_dev, blocks_row, height, breadth)
    panel_grad = jnp.einsum(
        "srbw,swv->srbv", panel_adjoint, low_inverse, preferred_element_type=jnp.float32
    ).astype(jnp.bfloat16)
    local_gram = jnp.einsum(
        "sbw,scw->bc", root_panels, root_panels, preferred_element_type=jnp.float32
    )
    root_total = lax.psum(local_gram, ("leaf", "sub"))
    root_adjoint = adjoint_block(root_block - root_total, root_cot)
    root_panel_adjoint = (
        -2.0
        * jnp.einsum("bc,scw->sbw", root_adjoint, root_panels, preferred_element_type=jnp.float32)
    ).astype(jnp.bfloat16)
    root_grad = jnp.einsum(
        "sbw,swv->sbv", root_panel_adjoint, low_inverse, preferred_element_type=jnp.float32
    ).astype(jnp.bfloat16)
    return (panel_grad, root_grad)


def solution(mesh):
    in_specs = (
        P(("leaf", "sub"), None, None, None),
        P(("leaf", "sub"), None, None),
        P(("leaf", "sub"), None, None),
        P(("leaf", "sub"), None),
        P(),
        P(("leaf", "sub"), None, None),
        P(("leaf", "sub"), None, None),
        P(),
        P(),
    )
    out_specs = (P(("leaf", "sub"), None, None, None), P(("leaf", "sub"), None, None))
    return jax.shard_map(body, mesh=mesh, in_specs=in_specs, out_specs=out_specs, check_vma=False)
```

profile of v0, /device:TPU:23, one launch (start us, length us, event | category | flops | bytes accessed | tf_op | source)
XLA Modules:
  0.0 601.4 jit_solution(2939340522287799899)
XLA Ops:
  10.0 3.0 broadcast_in_dim.46
  13.0 5.3 scatter_fusion
  18.3 13.1 %all-to-all-start = ((bf16[64,256,128]{2,1,0:T(8,128)(2,1)}), bf16[64,256,128]{2,1,0:T(8,128)(2,1)}, u32[]{:S(2)}, u32[]{:S(2)}) async-start(bf16[64,256,128]{2,1,0:T(8,128)(2,1)} %scatter_fusion), calls=%async_computation | async-start | bytes 8388608 | tf_op jit(solution)/shard_map/all_to_all | solution.py:51
  31.7 89.4 %all-to-all-done = bf16[64,256,128]{2,1,0:T(8,128)(2,1)} async-done(((bf16[64,256,128]{2,1,0:T(8,128)(2,1)}), bf16[64,256,128]{2,1,0:T(8,128)(2,1)}, u32[]{:S(2)}, u32[]{:S(2)}) %all-to-all-start) | async-done | bytes 4194336 | tf_op jit(solution)/shard_map/all_to_all | solution.py:51
  121.1 4.7 fusion.3
  126.0 11.7 %cholesky.130 = f32[128,128]{1,0:T(8,128)S(1)} custom-call(f32[128,128]{1,0:T(8,128)S(1)} %cholesky.194), custom_call_target="Cholesky" | custom-call | tf_op jit(solution)/shard_map/jit(cholesky)/cholesky | solution.py:8
  137.8 9.8 %custom-call.17 = f32[1,128,128]{1,2,0:T(8,128)S(1)} custom-call(f32[1,128,128]{2,1,0:T(8,128)S(1)} %get-tuple-element.47), custom_call_target="InvertDiagBlocksLowerTriangular" | custom-call | tf_op jit(solution)/shard_map/jit(cholesky)/cholesky | solution.py:8
  148.1 11.7 %cholesky.147 = f32[128,128]{1,0:T(8,128)S(1)} custom-call(f32[128,128]{1,0:T(8,128)S(1)} %convolution_subtract_fusion.3), custom_call_target="Cholesky" | custom-call | tf_op jit(solution)/shard_map/jit(cholesky)/cholesky | solution.py:8
  162.4 3.9 while.4
  163.0 1.4 bitcast_dynamic-update-slice_fusion.4
  165.0 1.4 bitcast_dynamic-update-slice_fusion.4
  166.4 31.4 %custom-call.18 = f32[2,128,128]{1,2,0:T(8,128)S(1)} custom-call(f32[2,128,128]{2,1,0:T(8,128)S(1)} %get-tuple-element.18), custom_call_target="InvertDiagBlocksLowerTriangular" | custom-call | tf_op jit(solution)/shard_map/jit(_solve_triangular)/triangular_solve | solution.py:10
  198.7 2.3 gather_fusion.1
  202.3 5.5 fusion
  207.7 12.5 %all-to-all-start.1 = ((bf16[64,256,128]{1,2,0:T(8,128)(2,1)}), bf16[64,256,128]{1,2,0:T(8,128)(2,1)}, u32[]{:S(2)}, u32[]{:S(2)}) async-start(bf16[64,256,128]{1,2,0:T(8,128)(2,1)} %fusion), calls=%async_computation.1 | async-start | bytes 8388608 | tf_op jit(solution)/shard_map/all_to_all | solution.py:58
  221.5 301.1 %all-reduce.3.cloned.1.call-done = f32[256,256]{0,1:T(8,128)} async-done(((f32[256,256]{0,1:T(8,128)}), f32[256,256]{0,1:T(8,128)}) %all-reduce.3.cloned.1.call-update) | async-done | bytes 262160 | tf_op jit(solution)/shard_map/psum | solution.py:67
  523.9 11.7 %cholesky.164 = f32[128,128]{1,0:T(8,128)S(1)} custom-call(f32[128,128]{1,0:T(8,128)S(1)} %cholesky.197), custom_call_target="Cholesky" | custom-call | tf_op jit(solution)/shard_map/jit(cholesky)/cholesky | solution.py:8
  535.6 9.8 %custom-call.19 = f32[1,128,128]{1,2,0:T(8,128)S(1)} custom-call(f32[1,128,128]{2,1,0:T(8,128)S(1)} %get-tuple-element.43), custom_call_target="InvertDiagBlocksLowerTriangular" | custom-call | tf_op jit(solution)/shard_map/jit(cholesky)/cholesky | solution.py:8
  545.9 11.7 %cholesky.181 = f32[128,128]{1,0:T(8,128)S(1)} custom-call(f32[128,128]{1,0:T(8,128)S(1)} %convolution_subtract_fusion.2), custom_call_target="Cholesky" | custom-call | tf_op jit(solution)/shard_map/jit(cholesky)/cholesky | solution.py:8
  559.6 4.0 while.5
  563.6 19.7 %custom-call.20 = f32[2,128,128]{1,2,0:T(8,128)S(1)} custom-call(f32[2,128,128]{2,1,0:T(8,128)S(1)} %get-tuple-element.19), custom_call_target="InvertDiagBlocksLowerTriangular" | custom-call | tf_op jit(solution)/shard_map/jit(_solve_triangular)/triangular_solve | solution.py:10
  583.8 2.3 gather_fusion.3
  589.5 2.8 gather_fusion.2
  592.4 1.8 convolution_convert_fusion
  (85 shorter events, 19.4 us)
Async XLA Ops:
  7.2 213.2 %copy-start = (bf16[6,256,128]{2,1,0:T(8,128)(2,1)S(1)}, bf16[6,256,128]{2,1,0:T(8,128)(2,1)}, u32[]{:S(2)}) copy-start(bf16[6,256,128]{2,1,0:T(8,128)(2,1)} %param.13) | copy-start | bytes 1179652
  7.2 5.8 copy-start.1
  18.3 13.1 %copy-start.3 = (f32[1,256,256]{2,1,0:T(8,128)S(1)}, f32[1,256,256]{2,1,0:T(8,128)}, u32[]{:S(2)}) copy-start(f32[1,256,256]{2,1,0:T(8,128)} %param.17) | copy-start | bytes 786436
  18.3 102.7 %all-to-all-start = ((bf16[64,256,128]{2,1,0:T(8,128)(2,1)}), bf16[64,256,128]{2,1,0:T(8,128)(2,1)}, u32[]{:S(2)}, u32[]{:S(2)}) async-start(bf16[64,256,128]{2,1,0:T(8,128)(2,1)} %scatter_fusion), calls=%async_computation | async-start | bytes 8388608 | tf_op jit(solution)/shard_map/all_to_all | solution.py:51
  31.7 130.1 %copy-start.5 = (f32[1,256,256]{2,1,0:T(8,128)S(1)}, f32[1,256,256]{2,1,0:T(8,128)}, u32[]{:S(2)}) copy-start(f32[1,256,256]{2,1,0:T(8,128)} %param.18) | copy-start | bytes 786436
  207.7 13.7 %copy-start.4 = (f32[256,256]{1,0:T(8,128)S(1)}, f32[256,256]{1,0:T(8,128)}, u32[]{:S(2)}) copy-start(f32[256,256]{1,0:T(8,128)} %param.19) | copy-start | bytes 786436
  207.7 381.8 %all-to-all-start.1 = ((bf16[64,256,128]{1,2,0:T(8,128)(2,1)}), bf16[64,256,128]{1,2,0:T(8,128)(2,1)}, u32[]{:S(2)}, u32[]{:S(2)}) async-start(bf16[64,256,128]{1,2,0:T(8,128)(2,1)} %fusion), calls=%async_computation.1 | async-start | bytes 8388608 | tf_op jit(solution)/shard_map/all_to_all | solution.py:58
  220.3 363.0 %copy-start.6 = (f32[256,256]{1,0:T(8,128)S(1)}, f32[256,256]{1,0:T(8,128)}, u32[]{:S(2)}) copy-start(f32[256,256]{1,0:T(8,128)} %param.20) | copy-start | bytes 786436
  220.3 302.4 %all-reduce.3.cloned.1.call-start = ((), (), s32[]{:S(2)}) async-start(), calls=%async_computation.2 | async-start | bytes 524288 | tf_op jit(solution)/shard_map/psum | solution.py:67
  523.8 64.5 %copy-start.2 = (bf16[6,128,128]{2,1,0:T(8,128)(2,1)S(1)}, bf16[6,128,128]{2,1,0:T(8,128)(2,1)}, u32[]{:S(2)}) copy-start(bf16[6,128,128]{2,1,0:T(8,128)(2,1)} %param.14) | copy-start | bytes 589828
Sparse Core Ops, SparseCore 0:
  226.7 295.9 all-reduce.2
where the time goes:
time: 612 us; the launch traced here: 601 us
  waiting for transfers between devices  391 us (64%)
  other arithmetic  120 us (20%)
  local copies, waits for them, and re-layouts  26.9 us (4%)
  starting transfers between devices  25.7 us (4%)
  matrix products  20.1 us (3%)
  between operations  17.4 us (3%)
    psum x1, waiting for transfers between devices, body(): root_total = lax.psum(local_gram, ('leaf', 'sub'))  301 us
    all_to_all x1, waiting for transfers between devices, body(): lax.all_to_all(outgoing, 'sub', split_axis=0, concat_axis=0, tiled=True)  89.4 us
    another operation x12, other arithmetic, adjoint_block(): factor = jnp.linalg.cholesky(schur)  67.9 us
    another operation x5, other arithmetic, adjoint_block(): inverse = jax.scipy.linalg.solve_triangular(factor, identity, lower=True)  51.2 us
    all_to_all x1, starting transfers between devices, body(): lax.all_to_all(outgoing, 'sub', split_axis=0, concat_axis=0, tiled=True)  13.1 us
    all_to_all x1, starting transfers between devices, body(): lax.all_to_all(answer, 'sub', split_axis=0, concat_axis=0, tiled=True)  12.5 us
  transfers between devices with their start and end apart: 3, of which 2 were waited for; matrix products, arithmetic and copies ran while one was open for 11% of the time, Pallas kernels for 0%

commit v1 on v0

--- a/solution.py
+++ b/solution.py
@@ -64,7 +64,7 @@
     local_gram = jnp.einsum(
         "sbw,scw->bc", root_panels, root_panels, preferred_element_type=jnp.float32
     )
-    root_total = lax.psum(local_gram, ("leaf", "sub"))
+    root_total = lax.psum(lax.psum(local_gram, "leaf"), "sub")
     root_adjoint = adjoint_block(root_block - root_total, root_cot)
     root_panel_adjoint = (
         -2.0

time: 612 us -> 591 us (0.966)
  the two profiles are of different devices: /device:TPU:23 before, /device:TPU:8 now
where the time goes in v1:
time: 591 us; the launch traced here: 581 us
  waiting for transfers between devices  377 us (64%)
  other arithmetic  121 us (20%)
  local copies, waits for them, and re-layouts  27 us (5%)
  matrix products  20.1 us (3%)
  starting transfers between devices  19.1 us (3%)
  between operations  17.4 us (3%)
    psum x2, waiting for transfers between devices, body(): root_total = lax.psum(lax.psum(local_gram, 'leaf'), 'sub')  280 us
    all_to_all x1, waiting for transfers between devices, body(): lax.all_to_all(outgoing, 'sub', split_axis=0, concat_axis=0, tiled=True)  96.9 us
    another operation x12, other arithmetic, adjoint_block(): factor = jnp.linalg.cholesky(schur)  67.9 us
    another operation x5, other arithmetic, adjoint_block(): inverse = jax.scipy.linalg.solve_triangular(factor, identity, lower=True)  51.2 us
    all_to_all x1, starting transfers between devices, body(): lax.all_to_all(outgoing, 'sub', split_axis=0, concat_axis=0, tiled=True)  13.5 us
  transfers between devices with their start and end apart: 4, of which 3 were waited for; matrix products, arithmetic and copies ran while one was open for 11% of the time, Pallas kernels for 0%

profile of v1, /device:TPU:8, one launch (start us, length us, event | category | flops | bytes accessed | tf_op | source)
XLA Modules:
  0.0 581.2 jit_solution(8455748455123213079)
XLA Ops:
  10.0 3.0 broadcast_in_dim.46
  13.0 5.4 scatter_fusion
  18.4 13.5 %all-to-all-start = ((bf16[64,256,128]{2,1,0:T(8,128)(2,1)}), bf16[64,256,128]{2,1,0:T(8,128)(2,1)}, u32[]{:S(2)}, u32[]{:S(2)}) async-start(bf16[64,256,128]{2,1,0:T(8,128)(2,1)} %scatter_fusion), calls=%async_computation | async-start | bytes 8388608 | tf_op jit(solution)/shard_map/all_to_all | solution.py:51
  32.0 96.9 %all-to-all-done = bf16[64,256,128]{2,1,0:T(8,128)(2,1)} async-done(((bf16[64,256,128]{2,1,0:T(8,128)(2,1)}), bf16[64,256,128]{2,1,0:T(8,128)(2,1)}, u32[]{:S(2)}, u32[]{:S(2)}) %all-to-all-start) | async-done | bytes 4194336 | tf_op jit(solution)/shard_map/all_to_all | solution.py:51
  128.9 4.7 fusion.3
  133.9 11.7 %cholesky.130 = f32[128,128]{1,0:T(8,128)S(1)} custom-call(f32[128,128]{1,0:T(8,128)S(1)} %cholesky.194), custom_call_target="Cholesky" | custom-call | tf_op jit(solution)/shard_map/jit(cholesky)/cholesky | solution.py:8
  145.6 9.8 %custom-call.17 = f32[1,128,128]{1,2,0:T(8,128)S(1)} custom-call(f32[1,128,128]{2,1,0:T(8,128)S(1)} %get-tuple-element.47), custom_call_target="InvertDiagBlocksLowerTriangular" | custom-call | tf_op jit(solution)/shard_map/jit(cholesky)/cholesky | solution.py:8
  155.9 11.7 %cholesky.147 = f32[128,128]{1,0:T(8,128)S(1)} custom-call(f32[128,128]{1,0:T(8,128)S(1)} %convolution_subtract_fusion.3), custom_call_target="Cholesky" | custom-call | tf_op jit(solution)/shard_map/jit(cholesky)/cholesky | solution.py:8
  170.3 3.9 while.4
  170.9 1.4 bitcast_dynamic-update-slice_fusion.4
  174.2 31.5 %custom-call.18 = f32[2,128,128]{1,2,0:T(8,128)S(1)} custom-call(f32[2,128,128]{2,1,0:T(8,128)S(1)} %get-tuple-element.18), custom_call_target="InvertDiagBlocksLowerTriangular" | custom-call | tf_op jit(solution)/shard_map/jit(_solve_triangular)/triangular_solve | solution.py:10
  206.6 2.3 gather_fusion.1
  210.1 5.5 fusion
  215.6 5.6 all-to-all-start.1
  222.3 118.6 %all-reduce.4.cloned.1.call-done = f32[256,256]{0,1:T(8,128)} async-done(((f32[256,256]{0,1:T(8,128)}), f32[256,256]{0,1:T(8,128)}) %all-reduce.4.cloned.1.call-update) | async-done | bytes 262160 | tf_op jit(solution)/shard_map/psum | solution.py:67
  341.1 161.3 %all-reduce.6.cloned.1.call-done = f32[256,256]{0,1:T(8,128)} async-done(((f32[256,256]{0,1:T(8,128)}), f32[256,256]{0,1:T(8,128)}) %all-reduce.6.cloned.1.call-update) | async-done | bytes 262160 | tf_op jit(solution)/shard_map/psum | solution.py:67
  503.6 11.7 %cholesky.164 = f32[128,128]{1,0:T(8,128)S(1)} custom-call(f32[128,128]{1,0:T(8,128)S(1)} %cholesky.197), custom_call_target="Cholesky" | custom-call | tf_op jit(solution)/shard_map/jit(cholesky)/cholesky | solution.py:8
  515.4 9.8 %custom-call.19 = f32[1,128,128]{1,2,0:T(8,128)S(1)} custom-call(f32[1,128,128]{2,1,0:T(8,128)S(1)} %get-tuple-element.43), custom_call_target="InvertDiagBlocksLowerTriangular" | custom-call | tf_op jit(solution)/shard_map/jit(cholesky)/cholesky | solution.py:8
  525.7 11.7 %cholesky.181 = f32[128,128]{1,0:T(8,128)S(1)} custom-call(f32[128,128]{1,0:T(8,128)S(1)} %convolution_subtract_fusion.2), custom_call_target="Cholesky" | custom-call | tf_op jit(solution)/shard_map/jit(cholesky)/cholesky | solution.py:8
  539.4 4.0 while.5
  543.4 19.7 %custom-call.20 = f32[2,128,128]{1,2,0:T(8,128)S(1)} custom-call(f32[2,128,128]{2,1,0:T(8,128)S(1)} %get-tuple-element.19), custom_call_target="InvertDiagBlocksLowerTriangular" | custom-call | tf_op jit(solution)/shard_map/jit(_solve_triangular)/triangular_solve | solution.py:10
  563.6 2.3 gather_fusion.3
  569.3 2.8 gather_fusion.2
  572.1 1.8 convolution_convert_fusion
  (88 shorter events, 20.8 us)
Async XLA Ops:
  7.2 214.1 %copy-start = (bf16[6,256,128]{2,1,0:T(8,128)(2,1)S(1)}, bf16[6,256,128]{2,1,0:T(8,128)(2,1)}, u32[]{:S(2)}) copy-start(bf16[6,256,128]{2,1,0:T(8,128)(2,1)} %param.13) | copy-start | bytes 1179652
  7.2 5.8 %copy-start.1 = (bf16[6,4,256,128]{3,2,1,0:T(8,128)(2,1)S(1)}, bf16[6,4,256,128]{3,2,1,0:T(8,128)(2,1)}, u32[]{:S(2)}) copy-start(bf16[6,4,256,128]{3,2,1,0:T(8,128)(2,1)} %param.12) | copy-start | bytes 4718596
  18.4 13.5 %copy-start.3 = (f32[1,256,256]{2,1,0:T(8,128)S(1)}, f32[1,256,256]{2,1,0:T(8,128)}, u32[]{:S(2)}) copy-start(f32[1,256,256]{2,1,0:T(8,128)} %param.17) | copy-start | bytes 786436
  18.4 110.6 %all-to-all-start = ((bf16[64,256,128]{2,1,0:T(8,128)(2,1)}), bf16[64,256,128]{2,1,0:T(8,128)(2,1)}, u32[]{:S(2)}, u32[]{:S(2)}) async-start(bf16[64,256,128]{2,1,0:T(8,128)(2,1)} %scatter_fusion), calls=%async_computation | async-start | bytes 8388608 | tf_op jit(solution)/shard_map/all_to_all | solution.py:51
  32.0 137.6 %copy-start.5 = (f32[1,256,256]{2,1,0:T(8,128)S(1)}, f32[1,256,256]{2,1,0:T(8,128)}, u32[]{:S(2)}) copy-start(f32[1,256,256]{2,1,0:T(8,128)} %param.18) | copy-start | bytes 786436
  215.6 125.4 %copy-start.4 = (f32[256,256]{1,0:T(8,128)S(1)}, f32[256,256]{1,0:T(8,128)}, u32[]{:S(2)}) copy-start(f32[256,256]{1,0:T(8,128)} %param.19) | copy-start | bytes 786436
  215.6 353.7 %all-to-all-start.1 = ((bf16[64,256,128]{1,2,0:T(8,128)(2,1)}), bf16[64,256,128]{1,2,0:T(8,128)(2,1)}, u32[]{:S(2)}, u32[]{:S(2)}) async-start(bf16[64,256,128]{1,2,0:T(8,128)(2,1)} %fusion), calls=%async_computation.1 | async-start | bytes 8388608 | tf_op jit(solution)/shard_map/all_to_all | solution.py:58
  221.2 341.9 %copy-start.6 = (f32[256,256]{1,0:T(8,128)S(1)}, f32[256,256]{1,0:T(8,128)}, u32[]{:S(2)}) copy-start(f32[256,256]{1,0:T(8,128)} %param.20) | copy-start | bytes 786436
  221.2 119.8 %all-reduce.4.cloned.1.call-start = ((), (), s32[]{:S(2)}) async-start(), calls=%async_computation.2 | async-start | bytes 524288 | tf_op jit(solution)/shard_map/psum | solution.py:67
  222.3 280.1 %all-reduce.6.cloned.1.call-start = ((), (), s32[]{:S(2)}) async-start(), calls=%async_computation.3 | async-start | bytes 524288 | tf_op jit(solution)/shard_map/psum | solution.py:67
  503.5 64.5 %copy-start.2 = (bf16[6,128,128]{2,1,0:T(8,128)(2,1)S(1)}, bf16[6,128,128]{2,1,0:T(8,128)(2,1)}, u32[]{:S(2)}) copy-start(bf16[6,128,128]{2,1,0:T(8,128)(2,1)} %param.14) | copy-start | bytes 589828
Sparse Core Ops, SparseCore 0:
  224.9 115.9 all-reduce.3
  344.8 157.5 all-reduce.5
